TPU v7x, 32 devices: a whole 2x2x4 slice. The times are simulated.
32 devices in a mesh: users: 16 (over z, x, core), ctx: 2 (over y).
Axes of the slice: x: 2, y: 2, z: 4, core: 2. Of those that a mesh axis runs over, the one named last changes fastest.
Arguments:
- events: bfloat16 [2048, 1024], P(('users', 'ctx')), may hold values from -6 to 6
- owner_id: int32 [2048, 1], P(('users', 'ctx')), may hold values from 0 to 15; in each aligned block of 64 rows (0 to 63, 64 to 127, ...) at most 6 rows name the same one
- event_bucket: int32 [2048], P(('users', 'ctx')), may hold values from 0 to 31
- cross_weight: bfloat16 [1024, 1024], P('users'), may hold values from -0.1875 to 0.1875
- cross_bias: float32 [1024], replicated, may hold values from -3 to 3
- project_weight: bfloat16 [1024, 4096], P('users'), may hold values from -0.1875 to 0.1875
- cache_keys: bfloat16 [16, 2048, 1024], P('users', 'ctx'), may hold values from -6 to 6
- cache_values: bfloat16 [16, 2048, 1024], P('users', 'ctx'), may hold values from -60 to 60
- cache_length: int32 [16], P('users'), may hold values from 256 to 2048
- cache_bucket: int32 [16, 2048], P('users', 'ctx'), may hold values from 0 to 31
- time_bias: float32 [32, 8], replicated, may hold values from -3 to 3
- norm_gain: float32 [1024], replicated, may hold values from 0.1 to 1.9
Outputs:
- gated: bfloat16 [2048, 1024], P(('users', 'ctx'))
Inputs may be any that keep to these rules, and one draw needn't show every extreme that they name: `owner_id`: no user is named by more than 6 of the 64 rows of one ingestion shard, and some user reaches that.
All inputs are finite; a program needn't handle non-finite values.
Results may differ from a plain program's by a relative error of at most 0.035.
Values may be sent and summed in bfloat16 or wider, within the bound.
No kernel may reach another device: no remote copies, remote signals or barrier semaphores. Data moves between devices by JAX's collectives and lax.ppermute only.
A program may use at most 64 MiB of HBM per device.

v0:
```python
import jax
import jax.numpy as jnp
from jax import lax
from jax.sharding import PartitionSpec as P

H = 8
norm_epsilon = 1e-05


def bias_table(buckets, time_bias):
    levels = jnp.arange(time_bias.shape[0], dtype=jnp.int32)
    picked = (buckets[:, None] == levels[None, :]).astype(jnp.float32)
    return jnp.dot(picked, time_bias, precision=lax.Precision.HIGHEST)


def weighted_sum(keys_part, values_part, queries, key_bias, allowed, scale_factor):
    scores = jnp.einsum("khd,qhd->hkq", keys_part, queries, preferred_element_type=jnp.float32)
    scores = scores * scale_factor + key_bias.T[:, :, None]
    weights = jnp.where(allowed, jax.nn.silu(scores), 0.0).astype(jnp.bfloat16)
    return jnp.einsum("hkq,khd->qhd", weights, values_part, preferred_element_type=jnp.float32)


def shards(
    events,
    owner_id,
    event_bucket,
    cross_weight,
    cross_bias,
    project_weight,
    cache_keys,
    cache_values,
    cache_length,
    cache_bucket,
    time_bias,
    norm_gain,
):
    row_count, feature_width = events.shape
    head_count = H
    head_width = feature_width // head_count
    owner_count = lax.axis_size("users")
    context_count = lax.axis_size("ctx")
    context_index = lax.axis_index("ctx")
    capacity = max(2, (3 * row_count + 2 * owner_count - 1) // (2 * owner_count))
    slot_count = owner_count * capacity
    cache_rows = cache_keys.shape[1]
    scale_factor = head_width ** (-0.5)
    source = events.astype(jnp.float32)
    cross_full = lax.all_gather(cross_weight, "users", axis=0, tiled=True)
    crossing = jnp.dot(events, cross_full, preferred_element_type=jnp.float32)
    crossed = (source * (crossing + cross_bias) + source).astype(jnp.bfloat16)
    owners = owner_id[:, 0]
    positions = jnp.arange(row_count, dtype=jnp.int32)
    earlier = (owners[None, :] == owners[:, None]) & (positions[None, :] < positions[:, None])
    ranking = jnp.sum(earlier.astype(jnp.int32), axis=1)
    slot_of_row = owners * capacity + ranking
    placing = jnp.arange(slot_count, dtype=jnp.int32)[:, None] == slot_of_row[None, :]
    placing_matrix = placing.astype(jnp.bfloat16)
    outgoing = jnp.dot(placing_matrix, crossed, preferred_element_type=jnp.float32).astype(
        jnp.bfloat16
    )
    labels = jnp.sum(jnp.where(placing, event_bucket[None, :] + 1, 0), axis=1).astype(jnp.bfloat16)
    arrived, arrived_labels = (
        lax.all_to_all(
            outgoing.reshape(owner_count, capacity, feature_width),
            "users",
            split_axis=0,
            concat_axis=0,
            tiled=True,
        ),
        lax.all_to_all(
            labels.reshape(owner_count, capacity), "users", split_axis=0, concat_axis=0, tiled=True
        ),
    )
    arrived = arrived.reshape(slot_count, feature_width)
    label_values = arrived_labels.reshape(slot_count).astype(jnp.int32)
    project_full = lax.all_gather(project_weight, "users", axis=0, tiled=True)
    projected = jnp.dot(arrived, project_full, preferred_element_type=jnp.float32)
    activated = jax.nn.silu(projected)
    gate_units = activated[:, :feature_width].astype(jnp.bfloat16)
    new_values = (
        activated[:, feature_width : 2 * feature_width]
        .astype(jnp.bfloat16)
        .reshape(slot_count, head_count, head_width)
    )
    new_queries = activated[:, 2 * feature_width : 3 * feature_width].astype(jnp.bfloat16)
    new_keys = (
        activated[:, 3 * feature_width :]
        .astype(jnp.bfloat16)
        .reshape(slot_count, head_count, head_width)
    )
    slot_index = jnp.arange(slot_count, dtype=jnp.int32)
    key_order = (
        slot_index // capacity * context_count + context_index
    ) * capacity + slot_index % capacity
    key_valid = label_values > 0
    new_bias = bias_table(jnp.maximum(label_values - 1, 0), time_bias)
    cache_key_heads = cache_keys[0].reshape(cache_rows, head_count, head_width)
    cache_value_heads = cache_values[0].reshape(cache_rows, head_count, head_width)
    cache_bias = bias_table(cache_bucket[0], time_bias)
    live_length = cache_length[0] - context_index * cache_rows
    cache_live = jnp.arange(cache_rows, dtype=jnp.int32) < live_length
    block_keys = min(256, cache_rows)
    block_total = cache_rows // block_keys

    def attend_block(query_rows, query_start):
        block_rows = query_rows.shape[0]
        queries = query_rows.reshape(block_rows, head_count, head_width)
        query_index = query_start + jnp.arange(block_rows, dtype=jnp.int32)
        query_context = query_index // slot_count
        query_slot = query_index % slot_count
        query_order = (
            query_slot // capacity * context_count + query_context
        ) * capacity + query_slot % capacity
        allowed = key_valid[None, :, None] & (
            key_order[None, :, None] <= query_order[None, None, :]
        )
        summed = weighted_sum(new_keys, new_values, queries, new_bias, allowed, scale_factor)

        def add_block(block_number, carried):
            offset = block_number * block_keys
            keys_part = lax.dynamic_slice_in_dim(cache_key_heads, offset, block_keys, 0)
            values_part = lax.dynamic_slice_in_dim(cache_value_heads, offset, block_keys, 0)
            bias_part = lax.dynamic_slice_in_dim(cache_bias, offset, block_keys, 0)
            live_part = lax.dynamic_slice_in_dim(cache_live, offset, block_keys, 0)
            return carried + weighted_sum(
                keys_part, values_part, queries, bias_part, live_part[None, :, None], scale_factor
            )

        summed = lax.fori_loop(0, block_total, add_block, summed)
        return summed.reshape(block_rows, feature_width)

    def attend(query_piece, start_row):
        piece_rows = query_piece.shape[0]
        if piece_rows > 512 and piece_rows % 512 == 0:
            block_count = piece_rows // 512
            stacked = query_piece.reshape(block_count, 512, feature_width)
            block_starts = start_row + 512 * jnp.arange(block_count, dtype=jnp.int32)

            def one_block(bundle):
                return attend_block(bundle[0], bundle[1])

            outputs = lax.map(one_block, (stacked, block_starts))
            return outputs.reshape(piece_rows, feature_width)
        return attend_block(query_piece, start_row)

    partials = attend(lax.all_gather(new_queries, "ctx", axis=0, tiled=True), jnp.int32(0))
    attended = lax.psum_scatter(
        partials.astype(jnp.bfloat16), "ctx", scatter_dimension=0, tiled=True
    ).astype(jnp.float32)
    center = jnp.mean(attended, axis=1, keepdims=True)
    spread = jnp.mean(jnp.square(attended - center), axis=1, keepdims=True)
    normed = (attended - center) * lax.rsqrt(spread + norm_epsilon)
    gated = (normed * norm_gain * gate_units.astype(jnp.float32)).astype(jnp.bfloat16)
    returned = lax.all_to_all(
        gated.reshape(owner_count, capacity, feature_width),
        "users",
        split_axis=0,
        concat_axis=0,
        tiled=True,
    )
    result = lax.dot_general(
        placing_matrix,
        returned.reshape(slot_count, feature_width),
        (((0,), (0,)), ((), ())),
        preferred_element_type=jnp.float32,
    )
    return result.astype(jnp.bfloat16)


def solution(mesh):
    return jax.shard_map(
        shards,
        mesh=mesh,
        in_specs=(
            P(("users", "ctx"), None),
            P(("users", "ctx"), None),
            P(("users", "ctx")),
            P("users", None),
            P(),
            P("users", None),
            P("users", "ctx", None),
            P("users", "ctx", None),
            P("users"),
            P("users", "ctx"),
            P(),
            P(),
        ),
        out_specs=P(("users", "ctx"), None),
        check_vma=False,
    )
```

profile of v0, /device:TPU:0, one launch (start us, length us, event | category | flops | bytes accessed | tf_op | source)
XLA Modules:
  0.0 193.8 jit_solution(14460470919051413623)
XLA Ops:
  6.5 0.0 copy-start
  6.5 0.0 all-gather.3.cloned.1.call-start
  6.5 0.7 all-gather.3.cloned.1.call-update
  7.3 0.0 all-gather.5.cloned.1.call-start
  7.3 0.7 all-gather.5.cloned.1.call-update
  8.0 0.9 convert_reduce_fusion.1
  8.9 0.7 broadcast_add_fusion
  9.6 0.7 multiply_add_fusion
  10.2 0.1 select_reduce_fusion
  10.4 0.7 convert_element_type.87
  11.1 7.4 %all-to-all-start.1 = ((bf16[16,1,6]{2,1,0:T(2,128)(2,1)}), bf16[16,1,6]{2,1,0:T(2,128)(2,1)S(1)}, u32[]{:S(2)}, u32[]{:S(2)}) async-start(bf16[16,1,6]{2,1,0:T(2,128)(2,1)} %convert_element_type.87), calls=%async_computation.1 | async-start | bytes 16384 | tf_op jit(solution)/shard_map/all_to_all | solution.py:70
  19.1 0.0 copy-done
  19.2 1.1 fusion.18
  20.3 0.0 copy-start.1
  20.3 4.1 %copy.45 = bf16[1,1024,1024]{1,2,0:T(8,128)(2,1)} copy(bf16[1,1024,1024]{2,1,0:T(8,128)(2,1)} %param.21) | data formatting | bytes 4194304 | tf_op args[7]
  24.4 0.0 copy-done.1
  24.4 0.0 copy-start.2
  24.4 0.0 copy-start.3
  24.4 2.6 %copy.46 = bf16[1,1024,1024]{1,2,0:T(8,128)(2,1)} copy(bf16[1,1024,1024]{2,1,0:T(8,128)(2,1)S(1)} %copy-done.1) | data formatting | bytes 4194304 | tf_op args[6]
  27.0 0.0 all-to-all-done.1
  27.1 0.1 gt.11
  27.2 0.1 max.11
  27.3 26.4 %all-gather.3.cloned.1.call-done = bf16[1024,1024]{1,0:T(8,128)(2,1)} async-done(((bf16[64,1024]{1,0:T(8,128)(2,1)}), bf16[1024,1024]{1,0:T(8,128)(2,1)}) %all-gather.3.cloned.1.call-update) | async-done | bytes 2097168 | tf_op jit(solution)/shard_map/all_gather | solution.py:48
  53.7 0.0 copy-done.2
  53.7 0.0 copy-done.3
  53.7 2.3 %convolution_convert_fusion = bf16[96,1024]{1,0:T(8,128)(2,1)S(1)} fusion(bf16[64,1024]{1,0:T(8,128)(2,1)S(1)} %copy-done.2, bf16[1024,1024]{1,0:T(8,128)(2,1)} %all-gather.3.cloned.1.call-done, f32[1024]{0:T(1024)S(1)} %copy-done.3, s32[64]{0:T(128)S(1)} %multiply_add_fusion), kind=kOutput, calls=%fused_computation.19 | convolution fusion | flops 147232768 | bytes 2429184 | tf_op jit(solution)/shard_map/dot_general | solution.py:58
  56.0 0.8 reshape.192
  56.7 3.5 %all-to-all-start = ((bf16[16,6,1024]{2,1,0:T(8,128)(2,1)}), bf16[16,6,1024]{2,1,0:T(8,128)(2,1)S(1)}, u32[]{:S(2)}, u32[]{:S(2)}) async-start(bf16[16,6,1024]{2,1,0:T(8,128)(2,1)} %reshape.192), calls=%async_computation | async-start | bytes 524288 | tf_op jit(solution)/shard_map/all_to_all | solution.py:63
  60.3 0.0 reduce-scatter.2.cloned.1.call-start
  60.3 0.2 convolution_bitcast_fusion.2
  60.5 0.2 compare_and_fusion
  60.7 11.9 %all-to-all-done = bf16[16,6,1024]{2,1,0:T(8,128)(2,1)S(1)} async-done(((bf16[16,6,1024]{2,1,0:T(8,128)(2,1)}), bf16[16,6,1024]{2,1,0:T(8,128)(2,1)S(1)}, u32[]{:S(2)}, u32[]{:S(2)}) %all-to-all-start) | async-done | bytes 196640 | tf_op jit(solution)/shard_map/all_to_all | solution.py:63
  72.6 0.1 reshape.193
  72.7 59.4 %all-gather.5.cloned.1.call-done = bf16[1024,4096]{1,0:T(8,128)(2,1)} async-done(((bf16[64,4096]{1,0:T(8,128)(2,1)}), bf16[1024,4096]{1,0:T(8,128)(2,1)}) %all-gather.5.cloned.1.call-update) | async-done | bytes 8388624 | tf_op jit(solution)/shard_map/all_gather | solution.py:76
  132.1 4.9 %multiply_convert_fusion = bf16[96,4096]{1,0:T(8,128)(2,1)S(1)} fusion(bf16[96,1024]{1,0:T(8,128)(2,1)S(1)} %reshape.193, bf16[1024,4096]{1,0:T(8,128)(2,1)} %all-gather.5.cloned.1.call-done), kind=kOutput, calls=%fused_computation.15 | convolution fusion | flops 807272448 | bytes 9371648 | tf_op jit(solution)/shard_map/dot_general | solution.py:77
  137.1 7.7 %all_gather.11 = bf16[192,1024]{1,0:T(8,128)(2,1)S(1)} all-gather(bf16[96,1024]{1,0:T(8,128)(2,1)S(1)} %get-tuple-element.172), channel_id=1, replica_groups=mesh['users'=16,'ctx'=2] {'ctx'}, dimensions={0}, use_global_device_ids=true | all-gather | bytes 589824 | tf_op jit(solution)/shard_map/all_gather | solution.py:146
  144.8 0.1 copy_bitcast_fusion.1
  144.9 0.7 convolution_bitcast_fusion.1
  145.6 9.1 %while.13 = (s32[]{:T(128)}, f32[192,8,128]{2,0,1:T(8,128)S(1)}, bf16[1024,8,128]{0,2,1:T(8,128)(2,1)}, pred[1024]{0:T(1024)(128)(4,1)S(1)}, bf16[1024,8,128]{0,...) while((s32[]{:T(128)}, f32[192,8,128]{2,0,1:T(8,128)S(1)}, ...), condition=%wide.region_3.4_spmd, body=%wide.region_2.3_spmd.sunk | while | flops 204668928 | bytes 3041187 | solution.py:129
  145.6 0.1 dynamic_slice.41
  145.7 2.2 %fusion.73 = f32[192,8,128]{2,0,1:T(8,128)S(1)} fusion(f32[192,8,128]{2,0,1:T(8,128)S(1)} %get-tuple-element.230, bf16[192,8,128]{2,0,1:T(8,128)(2,1)S(1)} %get-tuple-element.245, f32[8,256]{1,0:T(8,128)S(1)} %dynamic-slice_bitcast_fusion.2, pred[256]{0:T(512)(128)(4,1)S(1)} %dynamic_slice.41, bf16[1024,8,128]{0,2,1:T(8,128)(2,1)} %get-tuple-element.244, ...), kind=kOutput, calls=%fused_computation.2.clone.1 | convolution fusion | flops 204668928 | bytes 3024128 | tf_op jit(solution)/shard_map/while/body/eval_jaxpr/hkq,khd->qhd/dot_general | solution.py:20
  147.9 0.1 dynamic_slice.41
  148.0 2.1 %fusion.73 = f32[192,8,128]{2,0,1:T(8,128)S(1)} fusion(f32[192,8,128]{2,0,1:T(8,128)S(1)} %get-tuple-element.230, bf16[192,8,128]{2,0,1:T(8,128)(2,1)S(1)} %get-tuple-element.245, f32[8,256]{1,0:T(8,128)S(1)} %dynamic-slice_bitcast_fusion.2, pred[256]{0:T(512)(128)(4,1)S(1)} %dynamic_slice.41, bf16[1024,8,128]{0,2,1:T(8,128)(2,1)} %get-tuple-element.244, ...), kind=kOutput, calls=%fused_computation.2.clone.1 | convolution fusion | flops 204668928 | bytes 3024128 | tf_op jit(solution)/shard_map/while/body/eval_jaxpr/hkq,khd->qhd/dot_general | solution.py:20
  150.2 0.1 dynamic_slice.41
  150.3 2.2 %fusion.73 = f32[192,8,128]{2,0,1:T(8,128)S(1)} fusion(f32[192,8,128]{2,0,1:T(8,128)S(1)} %get-tuple-element.230, bf16[192,8,128]{2,0,1:T(8,128)(2,1)S(1)} %get-tuple-element.245, f32[8,256]{1,0:T(8,128)S(1)} %dynamic-slice_bitcast_fusion.2, pred[256]{0:T(512)(128)(4,1)S(1)} %dynamic_slice.41, bf16[1024,8,128]{0,2,1:T(8,128)(2,1)} %get-tuple-element.244, ...), kind=kOutput, calls=%fused_computation.2.clone.1 | convolution fusion | flops 204668928 | bytes 3024128 | tf_op jit(solution)/shard_map/while/body/eval_jaxpr/hkq,khd->qhd/dot_general | solution.py:20
  152.5 0.1 dynamic_slice.41
  152.5 2.1 %fusion.73 = f32[192,8,128]{2,0,1:T(8,128)S(1)} fusion(f32[192,8,128]{2,0,1:T(8,128)S(1)} %get-tuple-element.230, bf16[192,8,128]{2,0,1:T(8,128)(2,1)S(1)} %get-tuple-element.245, f32[8,256]{1,0:T(8,128)S(1)} %dynamic-slice_bitcast_fusion.2, pred[256]{0:T(512)(128)(4,1)S(1)} %dynamic_slice.41, bf16[1024,8,128]{0,2,1:T(8,128)(2,1)} %get-tuple-element.244, ...), kind=kOutput, calls=%fused_computation.2.clone.1 | convolution fusion | flops 204668928 | bytes 3024128 | tf_op jit(solution)/shard_map/while/body/eval_jaxpr/hkq,khd->qhd/dot_general | solution.py:20
  154.7 0.0 copy-start.4
  154.7 0.8 copy_bitcast_fusion
  155.5 0.0 reduce-scatter.2.cloned.1.call-update
  155.5 11.9 %reduce-scatter.2.cloned.1.call-done = bf16[96,1024]{1,0:T(8,128)(2,1)} async-done(((bf16[192,1024]{1,0:T(8,128)(2,1)}), bf16[96,1024]{1,0:T(8,128)(2,1)}) %reduce-scatter.2.cloned.1.call-update) | async-done | bytes 196624 | tf_op jit(solution)/shard_map/reduce_scatter | solution.py:147
  167.5 1.1 convert_reduce_fusion
  168.5 1.1 fusion.21
  169.7 0.0 copy-done.4
  169.7 1.1 fusion.24
  170.9 0.1 reshape.197
  170.9 15.4 %all_to_all.16 = bf16[16,6,1024]{2,1,0:T(8,128)(2,1)S(1)} all-to-all(bf16[16,6,1024]{2,1,0:T(8,128)(2,1)S(1)} %reshape.197), channel_id=1, replica_groups=mesh['users'=16,'ctx'=2] {'users'}, dimensions={0} | all-to-all | bytes 393216 | tf_op jit(solution)/shard_map/all_to_all | solution.py:154
  186.4 0.1 reshape.198
  186.4 0.9 convolution_convert_fusion.1
  (13 shorter events, 0.2 us)
Async XLA Ops:
  6.5 12.6 %copy-start = (f32[32,8]{0,1:T(8,128)S(1)}, f32[32,8]{0,1:T(8,128)}, u32[]{:S(2)}) copy-start(f32[32,8]{0,1:T(8,128)} %param.24) | copy-start | bytes 3076
  6.5 47.2 %all-gather.3.cloned.1.call-start = ((), (), s32[]{:S(2)}) async-start(), calls=%async_computation.4 | async-start | bytes 2228224 | tf_op jit(solution)/shard_map/all_gather | solution.py:48
  7.3 124.9 %all-gather.5.cloned.1.call-start = ((), (), s32[]{:S(2)}) async-start(), calls=%async_computation.5 | async-start | bytes 8912896 | tf_op jit(solution)/shard_map/all_gather | solution.py:76
  11.1 15.9 %all-to-all-start.1 = ((bf16[16,1,6]{2,1,0:T(2,128)(2,1)}), bf16[16,1,6]{2,1,0:T(2,128)(2,1)S(1)}, u32[]{:S(2)}, u32[]{:S(2)}) async-start(bf16[16,1,6]{2,1,0:T(2,128)(2,1)} %convert_element_type.87), calls=%async_computation.1 | async-start | bytes 16384 | tf_op jit(solution)/shard_map/all_to_all | solution.py:70
  20.3 4.1 %copy-start.1 = (bf16[1,1024,1024]{2,1,0:T(8,128)(2,1)S(1)}, bf16[1,1024,1024]{2,1,0:T(8,128)(2,1)}, u32[]{:S(2)}) copy-start(bf16[1,1024,1024]{2,1,0:T(8,128)(2,1)} %param.20) | copy-start | bytes 6291460
  24.4 29.3 %copy-start.2 = (bf16[64,1024]{1,0:T(8,128)(2,1)S(1)}, bf16[64,1024]{1,0:T(8,128)(2,1)}, u32[]{:S(2)}) copy-start(bf16[64,1024]{1,0:T(8,128)(2,1)} %param.14) | copy-start | bytes 393220
  24.4 29.3 %copy-start.3 = (f32[1024]{0:T(1024)S(1)}, f32[1024]{0:T(1024)}, u32[]{:S(2)}) copy-start(f32[1024]{0:T(1024)} %param.18) | copy-start | bytes 12292
  56.7 15.9 %all-to-all-start = ((bf16[16,6,1024]{2,1,0:T(8,128)(2,1)}), bf16[16,6,1024]{2,1,0:T(8,128)(2,1)S(1)}, u32[]{:S(2)}, u32[]{:S(2)}) async-start(bf16[16,6,1024]{2,1,0:T(8,128)(2,1)} %reshape.192), calls=%async_computation | async-start | bytes 524288 | tf_op jit(solution)/shard_map/all_to_all | solution.py:63
  60.3 107.2 %reduce-scatter.2.cloned.1.call-start = ((), (), s32[]{:S(2)}) async-start(), calls=%async_computation.6 | async-start | bytes 589824 | tf_op jit(solution)/shard_map/reduce_scatter | solution.py:147
  154.7 15.0 %copy-start.4 = (f32[1024]{0:T(1024)S(1)}, f32[1024]{0:T(1024)}, u32[]{:S(2)}) copy-start(f32[1024]{0:T(1024)} %param.25) | copy-start | bytes 12292
Sparse Core Ops, SparseCore 0:
  9.5 44.1 all-gather.2
  55.9 76.2 all-gather.4
  155.7 11.7 reduce-scatter.1
where the time goes:
time: 194 us
  waiting for transfers between devices  111 us (57%)
  blocking collectives  23.2 us (12%)
  matrix products  18.7 us (10%)
  between operations  13.9 us (7%)
  starting transfers between devices  11 us (6%)
  local copies, waits for them, and re-layouts  9.03 us (5%)
  other arithmetic  6.76 us (3%)
    all_gather x1, waiting for transfers between devices, shards(): project_full = lax.all_gather(project_weight, 'users', axis=0, tiled=True)  59.4 us
    all_gather x1, waiting for transfers between devices, shards(): cross_full = lax.all_gather(cross_weight, 'users', axis=0, tiled=True)  26.4 us
    all_to_all x1, blocking collectives, shards(): lax.all_to_all(gated.reshape(owner_count, capacity, feature_width), 'user...  15.4 us
    reduce_scatter x1, waiting for transfers between devices, shards(): lax.psum_scatter(partials.astype(jnp.bfloat16), 'ctx', scatter_dimension=...  11.9 us
    all_to_all x1, waiting for transfers between devices, shards(): lax.all_to_all(outgoing.reshape(owner_count, capacity, feature_width), 'u...  11.9 us
    dot_general x5, matrix products, weighted_sum(): jnp.einsum('hkq,khd->qhd', weights, values_part, preferred_element_type=j...  9.3 us
    all_gather x1, blocking collectives, shards(): lax.all_gather(new_queries, 'ctx', axis=0, tiled=True)  7.73 us
    all_to_all x1, starting transfers between devices, shards(): lax.all_to_all(labels.reshape(owner_count, capacity), 'users', split_axis...  7.39 us
  transfers between devices with their start and end apart: 5, of which 4 were waited for; matrix products, arithmetic and copies ran while one was open for 8% of the time, Pallas kernels for 0%

commit v1 on v0

--- a/solution.py
+++ b/solution.py
@@ -45,7 +45,14 @@
     cache_rows = cache_keys.shape[1]
     scale_factor = head_width ** (-0.5)
     source = events.astype(jnp.float32)
-    cross_full = lax.all_gather(cross_weight, "users", axis=0, tiled=True)
+    ring = [cross_weight]
+    for hop in range(15):
+        ring.append(lax.ppermute(ring[-1], "users", [(dev, (dev + 1) % 16) for dev in range(16)]))
+    cross_full = jnp.roll(
+        jnp.concatenate(ring[::-1], axis=0),
+        (lax.axis_index("users") + 1) * ring[0].shape[0],
+        axis=0,
+    )
     crossing = jnp.dot(events, cross_full, preferred_element_type=jnp.float32)
     crossed = (source * (crossing + cross_bias) + source).astype(jnp.bfloat16)
     owners = owner_id[:, 0]

time: 194 us -> 244 us (1.26)
  local copies, waits for them, and re-layouts: 9.03 us -> 39.1 us
  waiting for transfers between devices: 111 us -> 129 us
    ppermute x0 -> x15, waiting for transfers between devices: none -> 106 us  [shards(): lax.ppermute(ring[-1], 'users', [(dev, (dev + 1) % 16) for dev in range(1...]
    all_gather x1, waiting for transfers between devices: 59.4 us -> 0.02 us  [shards(): project_full = lax.all_gather(project_weight, 'users', axis=0, tiled=True)]
    unnamed x12 -> x55, local copies, waits for them, and re-layouts: 6.69 us -> 33.3 us
    all_gather x1 -> x0, waiting for transfers between devices: 26.4 us -> none  [shards(): cross_full = lax.all_gather(cross_weight, 'users', axis=0, tiled=True)]
    transpose x4, local copies, waits for them, and re-layouts: 0.03 us -> 2.81 us  [weighted_sum(): scores = scores * scale_factor + key_bias.T[:, :, None]]
  transfers between devices with their start and end apart: 5 -> 19, of which waited for: 4 -> 15; matrix products, arithmetic and copies ran while one was open for 8% -> 18% of each run, Pallas kernels for 0% -> 0%
where the time goes in v1:
time: 244 us; the launch traced here: 243 us
  waiting for transfers between devices  129 us (53%)
  local copies, waits for them, and re-layouts  39.1 us (16%)
  blocking collectives  22.8 us (9%)
  matrix products  19.3 us (8%)
  between operations  14.3 us (6%)
  starting transfers between devices  10.4 us (4%)
  other arithmetic  8.41 us (3%)
    ppermute x15, waiting for transfers between devices, shards(): lax.ppermute(ring[-1], 'users', [(dev, (dev + 1) % 16) for dev in range(1...  106 us
    unnamed x55, local copies, waits for them, and re-layouts  33.3 us
    all_to_all x1, blocking collectives, shards(): lax.all_to_all(gated.reshape(owner_count, capacity, feature_width), 'user...  15.4 us
    reduce_scatter x1, waiting for transfers between devices, shards(): lax.psum_scatter(partials.astype(jnp.bfloat16), 'ctx', scatter_dimension=...  12.2 us
    all_to_all x1, waiting for transfers between devices, shards(): lax.all_to_all(outgoing.reshape(owner_count, capacity, feature_width), 'u...  9.58 us
    dot_general x5, matrix products, weighted_sum(): jnp.einsum('hkq,khd->qhd', weights, values_part, preferred_element_type=j...  9.27 us
    all_gather x1, blocking collectives, shards(): lax.all_gather(new_queries, 'ctx', axis=0, tiled=True)  7.38 us
    all_to_all x1, starting transfers between devices, shards(): lax.all_to_all(labels.reshape(owner_count, capacity), 'users', split_axis...  5.82 us
  transfers between devices with their start and end apart: 19, of which 15 were waited for; matrix products, arithmetic and copies ran while one was open for 18% of the time, Pallas kernels for 0%

profile of v1, /device:TPU:0, one launch (start us, length us, event | category | flops | bytes accessed | tf_op | source)
XLA Modules:
  0.0 243.3 jit_solution(10379657266568347175)
XLA Ops:
  6.5 0.7 all-gather.2.cloned.1.call-update
  7.8 7.8 %collective-permute-done = bf16[64,1024]{1,0:T(8,128)(2,1)S(1)} collective-permute-done((bf16[64,1024]{1,0:T(8,128)(2,1)}, bf16[64,1024]{1,0:T(8,128)(2,1)S(1)}, u32[]{:S(2)}, u32[]{:S(2)}) %collective-permute-start) | collective-permute-done | bytes 131104 | tf_op jit(solution)/shard_map/ppermute | solution.py:50
  15.6 7.1 %collective-permute-done.1 = bf16[64,1024]{1,0:T(8,128)(2,1)S(1)} collective-permute-done((bf16[64,1024]{1,0:T(8,128)(2,1)S(1)}, bf16[64,1024]{1,0:T(8,128)(2,1)S(1)}, u32[]{:S(2)}, u32[]{:S(2)}) %collective-permute-start.1) | collective-permute-done | bytes 131104 | tf_op jit(solution)/shard_map/ppermute | solution.py:50
  22.7 10.0 %collective-permute-done.2 = bf16[64,1024]{1,0:T(8,128)(2,1)S(1)} collective-permute-done((bf16[64,1024]{1,0:T(8,128)(2,1)S(1)}, bf16[64,1024]{1,0:T(8,128)(2,1)S(1)}, u32[]{:S(2)}, u32[]{:S(2)}) %collective-permute-start.2) | collective-permute-done | bytes 131104 | tf_op jit(solution)/shard_map/ppermute | solution.py:50
  32.7 10.0 %collective-permute-done.3 = bf16[64,1024]{1,0:T(8,128)(2,1)S(1)} collective-permute-done((bf16[64,1024]{1,0:T(8,128)(2,1)S(1)}, bf16[64,1024]{1,0:T(8,128)(2,1)S(1)}, u32[]{:S(2)}, u32[]{:S(2)}) %collective-permute-start.3) | collective-permute-done | bytes 131104 | tf_op jit(solution)/shard_map/ppermute | solution.py:50
  42.8 7.1 %collective-permute-done.4 = bf16[64,1024]{1,0:T(8,128)(2,1)S(1)} collective-permute-done((bf16[64,1024]{1,0:T(8,128)(2,1)S(1)}, bf16[64,1024]{1,0:T(8,128)(2,1)S(1)}, u32[]{:S(2)}, u32[]{:S(2)}) %collective-permute-start.4) | collective-permute-done | bytes 131104 | tf_op jit(solution)/shard_map/ppermute | solution.py:50
  49.9 10.0 %collective-permute-done.5 = bf16[64,1024]{1,0:T(8,128)(2,1)S(1)} collective-permute-done((bf16[64,1024]{1,0:T(8,128)(2,1)S(1)}, bf16[64,1024]{1,0:T(8,128)(2,1)S(1)}, u32[]{:S(2)}, u32[]{:S(2)}) %collective-permute-start.5) | collective-permute-done | bytes 131104 | tf_op jit(solution)/shard_map/ppermute | solution.py:50
  59.9 10.0 %collective-permute-done.6 = bf16[64,1024]{1,0:T(8,128)(2,1)S(1)} collective-permute-done((bf16[64,1024]{1,0:T(8,128)(2,1)S(1)}, bf16[64,1024]{1,0:T(8,128)(2,1)S(1)}, u32[]{:S(2)}, u32[]{:S(2)}) %collective-permute-start.6) | collective-permute-done | bytes 131104 | tf_op jit(solution)/shard_map/ppermute | solution.py:50
  69.9 10.0 %collective-permute-done.7 = bf16[64,1024]{1,0:T(8,128)(2,1)S(1)} collective-permute-done((bf16[64,1024]{1,0:T(8,128)(2,1)S(1)}, bf16[64,1024]{1,0:T(8,128)(2,1)S(1)}, u32[]{:S(2)}, u32[]{:S(2)}) %collective-permute-start.7) | collective-permute-done | bytes 131104 | tf_op jit(solution)/shard_map/ppermute | solution.py:50
  79.9 10.0 %collective-permute-done.8 = bf16[64,1024]{1,0:T(8,128)(2,1)S(1)} collective-permute-done((bf16[64,1024]{1,0:T(8,128)(2,1)S(1)}, bf16[64,1024]{1,0:T(8,128)(2,1)S(1)}, u32[]{:S(2)}, u32[]{:S(2)}) %collective-permute-start.8) | collective-permute-done | bytes 131104 | tf_op jit(solution)/shard_map/ppermute | solution.py:50
  89.9 0.9 convert_reduce_fusion.1
  90.8 6.2 %collective-permute-done.9 = bf16[64,1024]{1,0:T(8,128)(2,1)S(1)} collective-permute-done((bf16[64,1024]{1,0:T(8,128)(2,1)S(1)}, bf16[64,1024]{1,0:T(8,128)(2,1)S(1)}, u32[]{:S(2)}, u32[]{:S(2)}) %collective-permute-start.9) | collective-permute-done | bytes 131104 | tf_op jit(solution)/shard_map/ppermute | solution.py:50
  97.0 0.7 multiply_add_fusion
  97.7 6.4 %collective-permute-done.10 = bf16[64,1024]{1,0:T(8,128)(2,1)S(1)} collective-permute-done((bf16[64,1024]{1,0:T(8,128)(2,1)S(1)}, bf16[64,1024]{1,0:T(8,128)(2,1)S(1)}, u32[]{:S(2)}, u32[]{:S(2)}) %collective-permute-start.10) | collective-permute-done | bytes 131104 | tf_op jit(solution)/shard_map/ppermute | solution.py:50
  104.9 0.7 convert_element_type.87
  105.6 5.8 %all-to-all-start.1 = ((bf16[16,1,6]{2,1,0:T(2,128)(2,1)}), bf16[16,1,6]{2,1,0:T(2,128)(2,1)S(1)}, u32[]{:S(2)}, u32[]{:S(2)}) async-start(bf16[16,1,6]{2,1,0:T(2,128)(2,1)} %convert_element_type.87), calls=%async_computation.1 | async-start | bytes 16384 | tf_op jit(solution)/shard_map/all_to_all | solution.py:77
  111.9 1.8 fusion.34
  114.2 4.7 %collective-permute-done.12 = bf16[64,1024]{1,0:T(8,128)(2,1)} collective-permute-done((bf16[64,1024]{1,0:T(8,128)(2,1)}, bf16[64,1024]{1,0:T(8,128)(2,1)}, u32[]{:S(2)}, u32[]{:S(2)}) %collective-permute-start.12) | collective-permute-done | bytes 131104 | tf_op jit(solution)/shard_map/ppermute | solution.py:50
  120.7 3.9 %copy.45 = bf16[1,1024,1024]{1,2,0:T(8,128)(2,1)} copy(bf16[1,1024,1024]{2,1,0:T(8,128)(2,1)} %param.21) | data formatting | bytes 4194304 | tf_op args[7]
  124.7 2.6 %copy.46 = bf16[1,1024,1024]{1,2,0:T(8,128)(2,1)} copy(bf16[1,1024,1024]{2,1,0:T(8,128)(2,1)S(1)} %copy-done.1) | data formatting | bytes 4194304 | tf_op args[6]
  127.6 7.0 %collective-permute-done.14 = bf16[64,1024]{1,0:T(8,128)(2,1)S(1)} collective-permute-done((bf16[64,1024]{1,0:T(8,128)(2,1)}, bf16[64,1024]{1,0:T(8,128)(2,1)S(1)}, u32[]{:S(2)}, u32[]{:S(2)}) %collective-permute-start.14) | collective-permute-done | bytes 131104 | tf_op jit(solution)/shard_map/ppermute | solution.py:50
  134.6 0.7 constant_dynamic-update-slice_fusion.31
  135.2 1.6 constant_dynamic-update-slice_fusion.30
  136.8 1.6 constant_dynamic-update-slice_fusion.29
  138.4 1.6 constant_dynamic-update-slice_fusion.28
  139.9 1.6 constant_dynamic-update-slice_fusion.27
  142.1 0.7 constant_dynamic-update-slice_fusion.25
  142.8 0.7 constant_dynamic-update-slice_fusion.24
  143.5 0.7 constant_dynamic-update-slice_fusion.23
  144.1 0.7 constant_dynamic-update-slice_fusion.22
  145.5 0.7 constant_dynamic-update-slice_fusion.20
  146.1 0.7 constant_dynamic-update-slice_fusion.19
  147.4 0.7 constant_dynamic-update-slice_fusion.17
  148.1 0.7 constant_dynamic-update-slice_fusion.16
  148.8 0.7 constant_dynamic-update-slice_fusion.15
  149.4 1.6 constant_dynamic-update-slice_fusion.14
  151.0 1.6 constant_dynamic-update-slice_fusion.13
  152.6 1.6 constant_dynamic-update-slice_fusion.12
  156.8 0.7 constant_dynamic-update-slice_fusion.7
  160.0 0.7 constant_dynamic-update-slice_fusion.2
  160.7 0.7 constant_dynamic-update-slice_fusion.1
  162.0 2.2 convolution_convert_fusion
  164.3 0.8 reshape.192
  165.0 3.5 %all-to-all-start = ((bf16[16,6,1024]{2,1,0:T(8,128)(2,1)}), bf16[16,6,1024]{2,1,0:T(8,128)(2,1)S(1)}, u32[]{:S(2)}, u32[]{:S(2)}) async-start(bf16[16,6,1024]{2,1,0:T(8,128)(2,1)} %reshape.192), calls=%async_computation | async-start | bytes 524288 | tf_op jit(solution)/shard_map/all_to_all | solution.py:70
  169.0 9.6 %all-to-all-done = bf16[16,6,1024]{2,1,0:T(8,128)(2,1)S(1)} async-done(((bf16[16,6,1024]{2,1,0:T(8,128)(2,1)}), bf16[16,6,1024]{2,1,0:T(8,128)(2,1)S(1)}, u32[]{:S(2)}, u32[]{:S(2)}) %all-to-all-start) | async-done | bytes 196640 | tf_op jit(solution)/shard_map/all_to_all | solution.py:70
  178.7 4.9 %multiply_convert_fusion = bf16[96,4096]{1,0:T(8,128)(2,1)S(1)} fusion(bf16[96,1024]{1,0:T(8,128)(2,1)S(1)} %reshape.193, bf16[1024,4096]{1,0:T(8,128)(2,1)} %all-gather.2.cloned.1.call-done), kind=kOutput, calls=%fused_computation.17 | convolution fusion | flops 807272448 | bytes 9371648 | tf_op jit(solution)/shard_map/dot_general | solution.py:84
  183.7 7.4 %all_gather.7 = bf16[192,1024]{1,0:T(8,128)(2,1)S(1)} all-gather(bf16[96,1024]{1,0:T(8,128)(2,1)S(1)} %get-tuple-element.172), channel_id=1, replica_groups=mesh['users'=16,'ctx'=2] {'ctx'}, dimensions={0}, use_global_device_ids=true | all-gather | bytes 589824 | tf_op jit(solution)/shard_map/all_gather | solution.py:153
  191.1 0.7 convolution_bitcast_fusion.1
  191.9 11.8 %while.13 = (s32[]{:T(128)}, f32[192,8,128]{2,0,1:T(8,128)S(1)}, bf16[1024,8,128]{0,2,1:T(8,128)(2,1)}, pred[1024]{0:T(1024)(128)(4,1)S(1)}, bf16[1024,8,128]{0,...) while((s32[]{:T(128)}, f32[192,8,128]{2,0,1:T(8,128)S(1)}, ...), condition=%wide.region_3.4_spmd, body=%wide.region_2.3_spmd.sunk | while | flops 204668928 | bytes 3041187 | solution.py:136
  191.9 0.7 dynamic-slice_bitcast_fusion.2
  192.7 2.1 fusion.90
  194.8 0.7 dynamic-slice_bitcast_fusion.2
  195.6 2.1 fusion.90
  197.8 0.7 dynamic-slice_bitcast_fusion.2
  198.5 2.1 fusion.90
  200.7 0.7 dynamic-slice_bitcast_fusion.2
  201.5 2.1 fusion.90
  203.7 0.8 copy_bitcast_fusion
  204.5 12.2 %reduce-scatter.2.cloned.1.call-done = bf16[96,1024]{1,0:T(8,128)(2,1)} async-done(((bf16[192,1024]{1,0:T(8,128)(2,1)}), bf16[96,1024]{1,0:T(8,128)(2,1)}) %reduce-scatter.2.cloned.1.call-update) | async-done | bytes 196624 | tf_op jit(solution)/shard_map/reduce_scatter | solution.py:154
  216.7 1.1 convert_reduce_fusion
  217.7 1.1 fusion.37
  218.9 1.1 fusion.40
  220.1 15.4 %all_to_all.16 = bf16[16,6,1024]{2,1,0:T(8,128)(2,1)S(1)} all-to-all(bf16[16,6,1024]{2,1,0:T(8,128)(2,1)S(1)} %reshape.197), channel_id=1, replica_groups=mesh['users'=16,'ctx'=2] {'users'}, dimensions={0} | all-to-all | bytes 393216 | tf_op jit(solution)/shard_map/all_to_all | solution.py:161
  235.6 0.9 convolution_convert_fusion.1
  (79 shorter events, 12.7 us)
Async XLA Ops:
  6.5 105.3 %copy-start = (f32[32,8]{0,1:T(8,128)S(1)}, f32[32,8]{0,1:T(8,128)}, u32[]{:S(2)}) copy-start(f32[32,8]{0,1:T(8,128)} %param.24) | copy-start | bytes 3076
  6.5 118.1 %copy-start.1 = (bf16[1,1024,1024]{2,1,0:T(8,128)(2,1)S(1)}, bf16[1,1024,1024]{2,1,0:T(8,128)(2,1)}, u32[]{:S(2)}) copy-start(bf16[1,1024,1024]{2,1,0:T(8,128)(2,1)} %param.20) | copy-start | bytes 6291460
  6.5 172.1 %all-gather.2.cloned.1.call-start = ((), (), s32[]{:S(2)}) async-start(), calls=%async_computation.4 | async-start | bytes 8912896 | tf_op jit(solution)/shard_map/all_gather | solution.py:83
  7.3 8.4 %collective-permute-start = (bf16[64,1024]{1,0:T(8,128)(2,1)}, bf16[64,1024]{1,0:T(8,128)(2,1)S(1)}, u32[]{:S(2)}, u32[]{:S(2)}) collective-permute-start(bf16[64,1024]{1,0:T(8,128)(2,1)} %param.17), channel_id=1, source_target_pairs={{0,2},{2,4},{4,6},{6,8},{8,10},{10,12},{12,14},{14,16},{16,18},{18... | collective-permute-start | bytes 393224 | tf_op jit(solution)/shard_map/ppermute | solution.py:50
  15.6 7.1 %collective-permute-start.1 = (bf16[64,1024]{1,0:T(8,128)(2,1)S(1)}, bf16[64,1024]{1,0:T(8,128)(2,1)S(1)}, u32[]{:S(2)}, u32[]{:S(2)}) collective-permute-start(bf16[64,1024]{1,0:T(8,128)(2,1)S(1)} %collective-permute-done), channel_id=1, source_target_pairs={{0,2},{2,4},{4,6},{6,8},{8,10},{10,12},{12,14},{14,16},{16,18},{18... | collective-permute-start | bytes 393224 | tf_op jit(solution)/shard_map/ppermute | solution.py:50
  22.7 10.0 %collective-permute-start.2 = (bf16[64,1024]{1,0:T(8,128)(2,1)S(1)}, bf16[64,1024]{1,0:T(8,128)(2,1)S(1)}, u32[]{:S(2)}, u32[]{:S(2)}) collective-permute-start(bf16[64,1024]{1,0:T(8,128)(2,1)S(1)} %collective-permute-done.1), channel_id=1, source_target_pairs={{0,2},{2,4},{4,6},{6,8},{8,10},{10,12},{12,14},{14,16},{16,18},{18... | collective-permute-start | bytes 393224 | tf_op jit(solution)/shard_map/ppermute | solution.py:50
  32.7 10.0 %collective-permute-start.3 = (bf16[64,1024]{1,0:T(8,128)(2,1)S(1)}, bf16[64,1024]{1,0:T(8,128)(2,1)S(1)}, u32[]{:S(2)}, u32[]{:S(2)}) collective-permute-start(bf16[64,1024]{1,0:T(8,128)(2,1)S(1)} %collective-permute-done.2), channel_id=1, source_target_pairs={{0,2},{2,4},{4,6},{6,8},{8,10},{10,12},{12,14},{14,16},{16,18},{18... | collective-permute-start | bytes 393224 | tf_op jit(solution)/shard_map/ppermute | solution.py:50
  42.8 7.1 %collective-permute-start.4 = (bf16[64,1024]{1,0:T(8,128)(2,1)S(1)}, bf16[64,1024]{1,0:T(8,128)(2,1)S(1)}, u32[]{:S(2)}, u32[]{:S(2)}) collective-permute-start(bf16[64,1024]{1,0:T(8,128)(2,1)S(1)} %collective-permute-done.3), channel_id=1, source_target_pairs={{0,2},{2,4},{4,6},{6,8},{8,10},{10,12},{12,14},{14,16},{16,18},{18... | collective-permute-start | bytes 393224 | tf_op jit(solution)/shard_map/ppermute | solution.py:50
  49.9 10.0 %collective-permute-start.5 = (bf16[64,1024]{1,0:T(8,128)(2,1)S(1)}, bf16[64,1024]{1,0:T(8,128)(2,1)S(1)}, u32[]{:S(2)}, u32[]{:S(2)}) collective-permute-start(bf16[64,1024]{1,0:T(8,128)(2,1)S(1)} %collective-permute-done.4), channel_id=1, source_target_pairs={{0,2},{2,4},{4,6},{6,8},{8,10},{10,12},{12,14},{14,16},{16,18},{18... | collective-permute-start | bytes 393224 | tf_op jit(solution)/shard_map/ppermute | solution.py:50
  59.9 10.0 %collective-permute-start.6 = (bf16[64,1024]{1,0:T(8,128)(2,1)S(1)}, bf16[64,1024]{1,0:T(8,128)(2,1)S(1)}, u32[]{:S(2)}, u32[]{:S(2)}) collective-permute-start(bf16[64,1024]{1,0:T(8,128)(2,1)S(1)} %collective-permute-done.5), channel_id=1, source_target_pairs={{0,2},{2,4},{4,6},{6,8},{8,10},{10,12},{12,14},{14,16},{16,18},{18... | collective-permute-start | bytes 393224 | tf_op jit(solution)/shard_map/ppermute | solution.py:50
  69.9 10.0 %collective-permute-start.7 = (bf16[64,1024]{1,0:T(8,128)(2,1)S(1)}, bf16[64,1024]{1,0:T(8,128)(2,1)S(1)}, u32[]{:S(2)}, u32[]{:S(2)}) collective-permute-start(bf16[64,1024]{1,0:T(8,128)(2,1)S(1)} %collective-permute-done.6), channel_id=1, source_target_pairs={{0,2},{2,4},{4,6},{6,8},{8,10},{10,12},{12,14},{14,16},{16,18},{18... | collective-permute-start | bytes 393224 | tf_op jit(solution)/shard_map/ppermute | solution.py:50
  79.9 10.0 %collective-permute-start.8 = (bf16[64,1024]{1,0:T(8,128)(2,1)S(1)}, bf16[64,1024]{1,0:T(8,128)(2,1)S(1)}, u32[]{:S(2)}, u32[]{:S(2)}) collective-permute-start(bf16[64,1024]{1,0:T(8,128)(2,1)S(1)} %collective-permute-done.7), channel_id=1, source_target_pairs={{0,2},{2,4},{4,6},{6,8},{8,10},{10,12},{12,14},{14,16},{16,18},{18... | collective-permute-start | bytes 393224 | tf_op jit(solution)/shard_map/ppermute | solution.py:50
  89.9 7.1 %collective-permute-start.9 = (bf16[64,1024]{1,0:T(8,128)(2,1)S(1)}, bf16[64,1024]{1,0:T(8,128)(2,1)S(1)}, u32[]{:S(2)}, u32[]{:S(2)}) collective-permute-start(bf16[64,1024]{1,0:T(8,128)(2,1)S(1)} %collective-permute-done.8), channel_id=1, source_target_pairs={{0,2},{2,4},{4,6},{6,8},{8,10},{10,12},{12,14},{14,16},{16,18},{18... | collective-permute-start | bytes 393224 | tf_op jit(solution)/shard_map/ppermute | solution.py:50
  97.0 7.1 %collective-permute-start.10 = (bf16[64,1024]{1,0:T(8,128)(2,1)S(1)}, bf16[64,1024]{1,0:T(8,128)(2,1)S(1)}, u32[]{:S(2)}, u32[]{:S(2)}) collective-permute-start(bf16[64,1024]{1,0:T(8,128)(2,1)S(1)} %collective-permute-done.9), channel_id=1, source_target_pairs={{0,2},{2,4},{4,6},{6,8},{8,10},{10,12},{12,14},{14,16},{16,18},{18... | collective-permute-start | bytes 393224 | tf_op jit(solution)/shard_map/ppermute | solution.py:50
  104.1 16.6 %copy-start.3 = (bf16[64,1024]{1,0:T(8,128)(2,1)}, bf16[64,1024]{1,0:T(8,128)(2,1)S(1)}, u32[]{:S(2)}) copy-start(bf16[64,1024]{1,0:T(8,128)(2,1)S(1)} %collective-permute-done.10) | copy-start | bytes 393220
  104.1 7.3 %collective-permute-start.11 = (bf16[64,1024]{1,0:T(8,128)(2,1)S(1)}, bf16[64,1024]{1,0:T(8,128)(2,1)}, u32[]{:S(2)}, u32[]{:S(2)}) collective-permute-start(bf16[64,1024]{1,0:T(8,128)(2,1)S(1)} %collective-permute-done.10), channel_id=1, source_target_pairs={{0,2},{2,4},{4,6},{6,8},{8,10},{10,12},{12,14},{14,16},{16,18},{18... | collective-permute-start | bytes 393224 | tf_op jit(solution)/shard_map/ppermute | solution.py:50
  105.6 21.7 %all-to-all-start.1 = ((bf16[16,1,6]{2,1,0:T(2,128)(2,1)}), bf16[16,1,6]{2,1,0:T(2,128)(2,1)S(1)}, u32[]{:S(2)}, u32[]{:S(2)}) async-start(bf16[16,1,6]{2,1,0:T(2,128)(2,1)} %convert_element_type.87), calls=%async_computation.1 | async-start | bytes 16384 | tf_op jit(solution)/shard_map/all_to_all | solution.py:77
  111.4 7.5 %collective-permute-start.12 = (bf16[64,1024]{1,0:T(8,128)(2,1)}, bf16[64,1024]{1,0:T(8,128)(2,1)}, u32[]{:S(2)}, u32[]{:S(2)}) collective-permute-start(bf16[64,1024]{1,0:T(8,128)(2,1)} %collective-permute-done.11), channel_id=1, source_target_pairs={{0,2},{2,4},{4,6},{6,8},{8,10},{10,12},{12,14},{14,16},{16,18},{18... | collective-permute-start | bytes 393224 | tf_op jit(solution)/shard_map/ppermute | solution.py:50
  118.9 8.3 %collective-permute-start.13 = (bf16[64,1024]{1,0:T(8,128)(2,1)}, bf16[64,1024]{1,0:T(8,128)(2,1)}, u32[]{:S(2)}, u32[]{:S(2)}) collective-permute-start(bf16[64,1024]{1,0:T(8,128)(2,1)} %collective-permute-done.12), channel_id=1, source_target_pairs={{0,2},{2,4},{4,6},{6,8},{8,10},{10,12},{12,14},{14,16},{16,18},{18... | collective-permute-start | bytes 393224 | tf_op jit(solution)/shard_map/ppermute | solution.py:50
  124.7 23.4 %copy-start.2 = (bf16[64,1024]{1,0:T(8,128)(2,1)S(1)}, bf16[64,1024]{1,0:T(8,128)(2,1)}, u32[]{:S(2)}) copy-start(bf16[64,1024]{1,0:T(8,128)(2,1)} %param.17) | copy-start | bytes 393220
  127.3 26.9 %copy-start.4 = (bf16[64,1024]{1,0:T(8,128)(2,1)S(1)}, bf16[64,1024]{1,0:T(8,128)(2,1)}, u32[]{:S(2)}) copy-start(bf16[64,1024]{1,0:T(8,128)(2,1)} %copy-done.3) | copy-start | bytes 393220
  127.3 7.3 %collective-permute-start.14 = (bf16[64,1024]{1,0:T(8,128)(2,1)}, bf16[64,1024]{1,0:T(8,128)(2,1)S(1)}, u32[]{:S(2)}, u32[]{:S(2)}) collective-permute-start(bf16[64,1024]{1,0:T(8,128)(2,1)} %collective-permute-done.13), channel_id=1, source_target_pairs={{0,2},{2,4},{4,6},{6,8},{8,10},{10,12},{12,14},{14,16},{16,18},{18... | collective-permute-start | bytes 393224 | tf_op jit(solution)/shard_map/ppermute | solution.py:50
  127.6 34.4 %copy-start.5 = (bf16[64,1024]{1,0:T(8,128)(2,1)S(1)}, bf16[64,1024]{1,0:T(8,128)(2,1)}, u32[]{:S(2)}) copy-start(bf16[64,1024]{1,0:T(8,128)(2,1)} %param.14) | copy-start | bytes 393220
  127.6 34.4 %copy-start.6 = (f32[1024]{0:T(1024)S(1)}, f32[1024]{0:T(1024)}, u32[]{:S(2)}) copy-start(f32[1024]{0:T(1024)} %param.18) | copy-start | bytes 12292
  146.8 22.0 %copy-start.8 = (s32[192]{0:T(256)S(1)}, s32[192]{0:T(256)}, u32[]{:S(2)}) copy-start(s32[192]{0:T(256)} %fusion.62) | copy-start | bytes 2308
  146.8 22.0 %copy-start.9 = (s32[96]{0:T(128)S(1)}, s32[96]{0:T(128)}, u32[]{:S(2)}) copy-start(s32[96]{0:T(128)} %fusion.64) | copy-start | bytes 1156
  165.0 13.5 %all-to-all-start = ((bf16[16,6,1024]{2,1,0:T(8,128)(2,1)}), bf16[16,6,1024]{2,1,0:T(8,128)(2,1)S(1)}, u32[]{:S(2)}, u32[]{:S(2)}) async-start(bf16[16,6,1024]{2,1,0:T(8,128)(2,1)} %reshape.192), calls=%async_computation | async-start | bytes 524288 | tf_op jit(solution)/shard_map/all_to_all | solution.py:70
  168.6 48.1 %reduce-scatter.2.cloned.1.call-start = ((), (), s32[]{:S(2)}) async-start(), calls=%async_computation.5 | async-start | bytes 589824 | tf_op jit(solution)/shard_map/reduce_scatter | solution.py:154
  183.6 8.2 %copy-start.10 = (pred[1024]{0:T(1024)(128)(4,1)S(1)}, pred[1024]{0:T(1024)(128)(4,1)}, u32[]{:S(2)}) copy-start(pred[1024]{0:T(1024)(128)(4,1)} %iota_compare_fusion.8) | copy-start | bytes 3076
  191.8 27.0 %copy-start.7 = (f32[1024]{0:T(1024)S(1)}, f32[1024]{0:T(1024)}, u32[]{:S(2)}) copy-start(f32[1024]{0:T(1024)} %param.25) | copy-start | bytes 12292
Sparse Core Ops, SparseCore 0:
  9.5 83.5 all-gather.1
  204.6 11.9 reduce-scatter.1
